TPU v7x, 128 devices: a whole 4x4x4 slice. The times are simulated.
128 devices in a mesh: sub: 32 (over x, y, core), rep: 4 (over z).
Axes of the slice: x: 4, y: 4, z: 4, core: 2. Of those that a mesh axis runs over, the one named last changes fastest.
Arguments:
- loads: bfloat16 [256, 256, 1024], P('sub', 'rep'), may hold values from -6 to 6
- operators: bfloat16 [256, 1024, 1024], P('sub'), may hold values from -0.1875 to 0.1875
- owner: int32 [2048, 1], P('sub'), may hold values from 0 to 31; in each aligned block of 64 rows (0 to 63, 64 to 127, ...) at most 4 rows name the same one
- dual_block: int32 [2048], P('sub'), may hold values from 0 to 15
- scale_index: int32 [65536], P('sub'), may hold values from 0 to 3
- basis: bfloat16 [65536, 1024], P('sub'), may hold values from -0.0234375 to 0.0234375
- coarse: bfloat16 [1024, 1024], replicated, may hold values from -1.5 to 1.5
Outputs:
- start: float32 [256, 65536], P('rep', 'sub')
- resid: float32 [256, 65536], P('rep', 'sub')
Inputs may be any that keep to these rules, and one draw needn't show every extreme that they name: Among the blocks of the subdomains of one index of sub (aligned blocks of 64 rows), no owner is named more than 4 times, a bound that some block reaches.
All inputs are finite; a program needn't handle non-finite values.
Results may differ from a plain program's by a relative error of at most 0.0075.
Values may be sent and summed in bfloat16 or wider, within the bound.
No kernel may reach another device: no remote copies, remote signals or barrier semaphores. Data moves between devices by JAX's collectives and lax.ppermute only.
A program may use at most 128 MiB of HBM per device.

v0:
```python
import jax
import jax.numpy as jnp
from jax import lax
from jax.sharding import PartitionSpec as P

BLK = 128


def apply_local(inputs, operators):
    return jnp.einsum("skl,slm->skm", inputs, operators, preferred_element_type=jnp.float32).astype(
        jnp.bfloat16
    )


def make_blocks(values, width):
    count, columns, local = values.shape
    return (
        values.reshape(count, columns, local // width, width)
        .transpose(0, 2, 1, 3)
        .reshape(-1, columns, width)
    )


def from_blocks(blocks, count):
    total, columns, width = blocks.shape
    per_sub = total // count
    return (
        blocks.reshape(count, per_sub, columns, width)
        .transpose(0, 2, 1, 3)
        .reshape(count, columns, per_sub * width)
    )


def pack_slots(blocks, dests, ranks, peers, slots):
    columns, width = (blocks.shape[1], blocks.shape[2])
    return jnp.zeros((peers, slots, columns, width), jnp.bfloat16).at[dests, ranks].set(blocks)


def accumulate(received, got_ids, own_blocks, weight):
    columns, width = (received.shape[2], received.shape[3])
    flat = received.reshape(-1, columns, width).astype(jnp.float32)
    total = jnp.zeros((own_blocks, columns, width), jnp.float32).at[got_ids.reshape(-1)].add(flat)
    return total.transpose(1, 0, 2).reshape(columns, own_blocks * width) * weight[None, :]


def per_device(loads, operators, owner, dual_block, scale_index, basis, coarse):
    sub_count = loads.shape[0]
    width = BLK
    peers = lax.axis_size("sub")
    dests = owner[:, 0]
    nblocks = dests.shape[0]
    slots = max(2, 2 * nblocks // peers)
    own_blocks = basis.shape[0] // width
    positions = jnp.arange(nblocks, dtype=jnp.int32)
    earlier = positions[None, :] < positions[:, None]
    same = dests[None, :] == dests[:, None]
    ranks = jnp.sum(jnp.logical_and(earlier, same), axis=1)
    weight = 1.0 / (1.0 + scale_index.astype(jnp.float32))
    terms = apply_local(loads, operators)
    packed = pack_slots(make_blocks(terms, width), dests, ranks, peers, slots)
    id_slots = jnp.zeros((peers, slots), jnp.int32).at[dests, ranks].set(dual_block)
    received, got_ids = (
        lax.all_to_all(packed, "sub", split_axis=0, concat_axis=0, tiled=True),
        lax.all_to_all(id_slots, "sub", split_axis=0, concat_axis=0, tiled=True),
    )
    dual = accumulate(received, got_ids, own_blocks, weight)
    coeff = jnp.dot(dual.astype(jnp.bfloat16), basis, preferred_element_type=jnp.float32)
    summed = lax.psum(coeff, "sub")
    solved = jnp.dot(
        summed.astype(jnp.bfloat16), coarse, preferred_element_type=jnp.float32
    ).astype(jnp.bfloat16)
    start = lax.dot_general(
        solved, basis, (((1,), (1,)), ((), ())), preferred_element_type=jnp.float32
    )
    columns = start.shape[0]
    start_blocks = start.astype(jnp.bfloat16).reshape(columns, own_blocks, width).transpose(1, 0, 2)
    requested = start_blocks[got_ids]
    returned = lax.all_to_all(requested, "sub", split_axis=0, concat_axis=0, tiled=True)
    picked = returned[dests, ranks]
    local = from_blocks(picked, sub_count)
    again = apply_local(local, operators)
    received_again = lax.all_to_all(
        pack_slots(make_blocks(again, width), dests, ranks, peers, slots),
        "sub",
        split_axis=0,
        concat_axis=0,
        tiled=True,
    )
    applied = accumulate(received_again, got_ids, own_blocks, weight)
    return (start, dual - applied)


def solution(mesh):
    return jax.shard_map(
        per_device,
        mesh=mesh,
        in_specs=(
            P("sub", "rep", None),
            P("sub", None, None),
            P("sub", None),
            P("sub"),
            P("sub"),
            P("sub", None),
            P(),
        ),
        out_specs=(P("rep", "sub"), P("rep", "sub")),
        check_vma=False,
    )
```

profile of v0, /device:TPU:1, one launch (start us, length us, event | category | flops | bytes accessed | tf_op | source)
XLA Modules:
  0.0 336.0 jit_solution(8166071477639882503)
XLA Ops:
  0.6 0.0 copy-start
  0.6 1.0 convert_reduce_fusion
  1.6 0.7 fusion.15
  2.3 5.7 %scatter_fusion = s32[32,4]{0,1:T(4,128)S(1)} fusion(s32[32,4]{0,1:T(4,128)S(1)} %broadcast.75, s32[64]{0:T(128)S(1)} %get-tuple-element.2, s32[64]{0:T(128)} %param.10), kind=kCustom, calls=%fused_computation.2 | custom fusion | bytes 1280 | tf_op jit(solution)/shard_map/scatter | solution.py:61
  8.1 0.7 copy.33
  8.8 8.6 %all-to-all-start = ((s32[32,1,4]{2,1,0:T(1,128)}), s32[32,1,4]{2,1,0:T(1,128)S(1)}, u32[]{:S(2)}, u32[]{:S(2)}) async-start(s32[32,1,4]{2,1,0:T(1,128)} %copy.33), calls=%async_computation | async-start | bytes 32768 | tf_op jit(solution)/shard_map/all_to_all | solution.py:64
  17.4 9.1 %fusion = bf16[8,8,8,8,128]{4,3,2,1,0:T(8,128)(2,1)S(1)} fusion(bf16[8,64,1024]{2,1,0:T(8,128)(2,1)} %param.7, bf16[8,1024,1024]{2,1,0:T(8,128)(2,1)} %param.8), kind=kOutput, calls=%fused_computation.11 | convolution fusion | flops 1074266112 | bytes 18874368 | tf_op jit(solution)/shard_map/skl,slm->skm/dot_general | solution.py:10
  26.5 0.3 copy.63
  26.8 1.9 broadcast.81.clone
  28.7 8.9 %scatter_fusion.1 = bf16[32,4,64,128]{3,2,1,0:T(8,128)(2,1)} fusion(bf16[32,4,64,128]{3,2,1,0:T(8,128)(2,1)} %broadcast.81.clone, s32[64]{0:T(128)S(1)} %get-tuple-element.2, bf16[64,64,128]{2,1,0:T(8,128)(2,1)S(1)} %bitcast.87), kind=kCustom, calls=%fused_computation.3 | custom fusion | bytes 3146240 | tf_op jit(solution)/shard_map/scatter | solution.py:36
  37.5 0.0 copy-start.1
  37.5 0.0 all-to-all-done
  37.5 7.6 %all-to-all-start.1 = ((bf16[32,4,64,128]{3,2,1,0:T(8,128)(2,1)}), bf16[32,4,64,128]{3,2,1,0:T(8,128)(2,1)}, u32[]{:S(2)}, u32[]{:S(2)}) async-start(bf16[32,4,64,128]{3,2,1,0:T(8,128)(2,1)} %scatter_fusion.1), calls=%async_computation.1 | async-start | bytes 4194304 | tf_op jit(solution)/shard_map/all_to_all | solution.py:63
  45.1 0.0 copy-done.1
  45.1 0.5 broadcast.184
  45.7 0.7 reduce.3
  46.4 0.1 reshape.115
  46.5 0.1 copy.37
  46.5 0.1 copy.38
  46.6 0.1 reshape.129
  46.8 26.7 %all-to-all-done.1 = bf16[32,4,64,128]{3,2,1,0:T(8,128)(2,1)} async-done(((bf16[32,4,64,128]{3,2,1,0:T(8,128)(2,1)}), bf16[32,4,64,128]{3,2,1,0:T(8,128)(2,1)}, u32[]{:S(2)}, u32[]{:S(2)}) %all-to-all-start.1) | async-done | bytes 2097184 | tf_op jit(solution)/shard_map/all_to_all | solution.py:63
  73.5 4.0 %bitcast_convert_fusion.1 = f32[128,64,128]{2,1,0:T(8,128)} fusion(bf16[32,4,64,128]{3,2,1,0:T(8,128)(2,1)} %all-to-all-done.1), kind=kLoop, calls=%fused_computation.8 | loop fusion | flops 1048576 | bytes 6291456 | tf_op jit(solution)/shard_map/convert_element_type | solution.py:41
  77.5 13.5 %scatter_fusion.2 = f32[16,64,128]{2,1,0:T(8,128)S(1)} fusion(f32[16,64,128]{2,1,0:T(8,128)S(1)} %broadcast.74.clone, s32[128]{0:T(128)S(1)} %fusion.14, f32[128,64,128]{2,1,0:T(8,128)} %bitcast_convert_fusion.1), kind=kCustom, calls=%fused_computation.4 | custom fusion | flops 1048576 | bytes 12583424 | tf_op jit(solution)/shard_map/scatter-add | solution.py:42
  91.1 3.0 fusion.7
  94.1 121.1 %all-reduce.1 = bf16[64,1024]{1,0:T(8,128)(2,1)S(1)} all-reduce(f32[64,1024]{1,0:T(8,128)S(1)} %fusion.7), channel_id=1, replica_groups=mesh['sub'=32,'rep'=4] {'sub'}, use_global_device_ids=true, to_apply=%region_4.0 | all-reduce | flops 65536 | bytes 393216 | tf_op jit(solution)/shard_map/psum | solution.py:68
  215.3 0.0 copy-done
  215.3 4.8 %fusion.2 = f32[64,2048]{1,0:T(8,128)} fusion(bf16[2048,1024]{1,0:T(8,128)(2,1)} %param.12, bf16[1024,1024]{1,0:T(8,128)(2,1)S(1)} %copy-done, bf16[64,1024]{1,0:T(8,128)(2,1)S(1)} %all-reduce.1), kind=kOutput, calls=%fused_computation.14 | convolution fusion | flops 402718720 | bytes 6946816 | tf_op jit(solution)/shard_map/dot_general | solution.py:72
  220.0 1.1 bitcast_bitcast_fusion
  221.1 2.1 gather_fusion
  223.2 38.3 %all_to_all.27 = bf16[32,4,64,128]{3,2,1,0:T(8,128)(2,1)} all-to-all(bf16[32,4,64,128]{3,2,1,0:T(8,128)(2,1)} %bitcast.85), channel_id=1, replica_groups=mesh['sub'=32,'rep'=4] {'sub'}, dimensions={0} | all-to-all | bytes 4194304 | tf_op jit(solution)/shard_map/all_to_all | solution.py:78
  261.5 3.3 gather_fusion.1
  264.8 9.1 %fusion.1 = bf16[8,8,8,8,128]{4,3,2,1,0:T(8,128)(2,1)S(1)} fusion(bf16[8,1024,1024]{2,1,0:T(8,128)(2,1)} %param.8, bf16[8,8,8,8,128]{4,3,2,1,0:T(8,128)(2,1)} %bitcast.88), kind=kOutput, calls=%fused_computation.12 | convolution fusion | flops 1074266112 | bytes 18874368 | tf_op jit(solution)/shard_map/skl,slm->skm/dot_general | solution.py:10
  273.9 1.3 copy.62
  275.2 1.9 broadcast.81
  277.1 9.8 %scatter_fusion.3 = bf16[32,4,64,128]{3,2,1,0:T(8,128)(2,1)} fusion(bf16[32,4,64,128]{3,2,1,0:T(8,128)(2,1)} %broadcast.81, s32[64]{0:T(128)S(1)} %get-tuple-element.2, bf16[64,64,128]{2,1,0:T(8,128)(2,1)} %bitcast.86), kind=kCustom, calls=%fused_computation.5 | custom fusion | bytes 3146240 | tf_op jit(solution)/shard_map/scatter | solution.py:36
  286.9 32.1 %all_to_all.28 = bf16[32,4,64,128]{3,2,1,0:T(8,128)(2,1)S(1)} all-to-all(bf16[32,4,64,128]{3,2,1,0:T(8,128)(2,1)} %scatter_fusion.3), channel_id=1, replica_groups=mesh['sub'=32,'rep'=4] {'sub'}, dimensions={0} | all-to-all | bytes 4194304 | tf_op jit(solution)/shard_map/all_to_all | solution.py:82
  319.0 2.5 bitcast_convert_fusion
  321.6 13.5 %scatter_fusion.4 = f32[16,64,128]{2,1,0:T(8,128)S(1)} fusion(f32[16,64,128]{2,1,0:T(8,128)S(1)} %broadcast.74, s32[128]{0:T(128)S(1)} %fusion.14, f32[128,64,128]{2,1,0:T(8,128)} %bitcast_convert_fusion), kind=kCustom, calls=%fused_computation.6 | custom fusion | flops 1048576 | bytes 12583424 | tf_op jit(solution)/shard_map/scatter-add | solution.py:42
  335.1 0.9 fusion.5
  (7 shorter events, 0.1 us)
Async XLA Ops:
  0.6 214.6 %copy-start = (bf16[1024,1024]{1,0:T(8,128)(2,1)S(1)}, bf16[1024,1024]{1,0:T(8,128)(2,1)}, u32[]{:S(2)}) copy-start(bf16[1024,1024]{1,0:T(8,128)(2,1)} %param.13) | copy-start | bytes 6291460
  8.8 28.8 %all-to-all-start = ((s32[32,1,4]{2,1,0:T(1,128)}), s32[32,1,4]{2,1,0:T(1,128)S(1)}, u32[]{:S(2)}, u32[]{:S(2)}) async-start(s32[32,1,4]{2,1,0:T(1,128)} %copy.33), calls=%async_computation | async-start | bytes 32768 | tf_op jit(solution)/shard_map/all_to_all | solution.py:64
  37.5 7.6 %copy-start.1 = (s32[2048]{0:T(1024)S(1)}, s32[2048]{0:T(1024)}, u32[]{:S(2)}) copy-start(s32[2048]{0:T(1024)} %param.11) | copy-start | bytes 24580
  37.5 35.9 %all-to-all-start.1 = ((bf16[32,4,64,128]{3,2,1,0:T(8,128)(2,1)}), bf16[32,4,64,128]{3,2,1,0:T(8,128)(2,1)}, u32[]{:S(2)}, u32[]{:S(2)}) async-start(bf16[32,4,64,128]{3,2,1,0:T(8,128)(2,1)} %scatter_fusion.1), calls=%async_computation.1 | async-start | bytes 4194304 | tf_op jit(solution)/shard_map/all_to_all | solution.py:63
where the time goes:
time: 338 us; the launch traced here: 336 us
  blocking collectives  192 us (57%)
  other arithmetic  37.9 us (11%)
  local copies, waits for them, and re-layouts  36.8 us (11%)
  waiting for transfers between devices  26.7 us (8%)
  matrix products  26.1 us (8%)
  starting transfers between devices  16.2 us (5%)
    psum x1, blocking collectives, per_device(): summed = lax.psum(coeff, 'sub')  121 us
    all_to_all x1, blocking collectives, per_device(): lax.all_to_all(requested, 'sub', split_axis=0, concat_axis=0, tiled=True)  38.3 us
    all_to_all x1, blocking collectives, per_device(): lax.all_to_all(pack_slots(make_blocks(again, width), dests, ranks, peers,...  32.1 us
    scatter-add x2, other arithmetic, accumulate(): jnp.zeros((own_blocks, columns, width), jnp.float32).at[got_ids.reshape(-1)]  27.1 us
    all_to_all x1, waiting for transfers between devices, per_device(): lax.all_to_all(packed, 'sub', split_axis=0, concat_axis=0, tiled=True)  26.7 us
    scatter x2, local copies, waits for them, and re-layouts, pack_slots(): jnp.zeros((peers, slots, columns, width), jnp.bfloat16).at[dests, ranks]  18.7 us
    dot_general x2, matrix products, apply_local(): jnp.einsum('skl,slm->skm', inputs, operators, preferred_element_type=jnp....  18.3 us
    all_to_all x1, starting transfers between devices, per_device(): lax.all_to_all(id_slots, 'sub', split_axis=0, concat_axis=0, tiled=True)  8.59 us
  transfers between devices with their start and end apart: 2, of which 1 were waited for; matrix products, arithmetic and copies ran while one was open for 6% of the time, Pallas kernels for 0%

commit v1 on v0

--- a/solution.py
+++ b/solution.py
@@ -4,6 +4,10 @@
 from jax.sharding import PartitionSpec as P
 
 BLK = 128
+
+
+def panels_create(axis_tag, a0):
+    return jnp.sum(lax.all_gather(a0, axis_tag), 0)
 
 
 def apply_local(inputs, operators):
@@ -65,7 +69,7 @@
     )
     dual = accumulate(received, got_ids, own_blocks, weight)
     coeff = jnp.dot(dual.astype(jnp.bfloat16), basis, preferred_element_type=jnp.float32)
-    summed = lax.psum(coeff, "sub")
+    summed = panels_create("sub", coeff)
     solved = jnp.dot(
         summed.astype(jnp.bfloat16), coarse, preferred_element_type=jnp.float32
     ).astype(jnp.bfloat16)

time: 338 us -> 282 us (0.83)
  blocking collectives: 192 us -> 65.8 us
  waiting for transfers between devices: 26.7 us -> 78.5 us
  between operations: 0.79 us -> 14.2 us
    psum x1 -> x0, blocking collectives: 121 us -> none  [per_device(): summed = lax.psum(coeff, 'sub')]
    all_gather x0 -> x1, waiting for transfers between devices: none -> 51.5 us  [panels_create(): return jnp.sum(lax.all_gather(a0, axis_tag), 0)]
    all_to_all x1, blocking collectives: 38.3 us -> 33.7 us  [per_device(): lax.all_to_all(requested, 'sub', split_axis=0, concat_axis=0, tiled=True)]
    reduce_sum x0 -> x1, other arithmetic: none -> 4.01 us  [panels_create(): return jnp.sum(lax.all_gather(a0, axis_tag), 0)]
  transfers between devices with their start and end apart: 2 -> 3, of which waited for: 1 -> 2; matrix products, arithmetic and copies ran while one was open for 6% -> 8% of each run, Pallas kernels for 0% -> 0%
where the time goes in v1:
time: 282 us; the launch traced here: 280 us
  waiting for transfers between devices  78.5 us (28%)
  blocking collectives  65.8 us (23%)
  other arithmetic  40.9 us (15%)
  local copies, waits for them, and re-layouts  38.8 us (14%)
  matrix products  26 us (9%)
  starting transfers between devices  16.1 us (6%)
  between operations  14.2 us (5%)
    all_gather x1, waiting for transfers between devices, panels_create(): return jnp.sum(lax.all_gather(a0, axis_tag), 0)  51.5 us
    all_to_all x1, blocking collectives, per_device(): lax.all_to_all(requested, 'sub', split_axis=0, concat_axis=0, tiled=True)  33.7 us
    all_to_all x1, blocking collectives, per_device(): lax.all_to_all(pack_slots(make_blocks(again, width), dests, ranks, peers,...  32.1 us
    scatter-add x2, other arithmetic, accumulate(): jnp.zeros((own_blocks, columns, width), jnp.float32).at[got_ids.reshape(-1)]  27.1 us
    all_to_all x1, waiting for transfers between devices, per_device(): lax.all_to_all(packed, 'sub', split_axis=0, concat_axis=0, tiled=True)  27 us
    scatter x2, local copies, waits for them, and re-layouts, pack_slots(): jnp.zeros((peers, slots, columns, width), jnp.bfloat16).at[dests, ranks]  19.6 us
    dot_general x2, matrix products, apply_local(): jnp.einsum('skl,slm->skm', inputs, operators, preferred_element_type=jnp....  18.3 us
    all_to_all x1, starting transfers between devices, per_device(): lax.all_to_all(id_slots, 'sub', split_axis=0, concat_axis=0, tiled=True)  8.59 us
  transfers between devices with their start and end apart: 3, of which 2 were waited for; matrix products, arithmetic and copies ran while one was open for 8% of the time, Pallas kernels for 0%

profile of v1, /device:TPU:1, one launch (start us, length us, event | category | flops | bytes accessed | tf_op | source)
XLA Modules:
  0.0 280.2 jit_solution(17387380930353697383)
XLA Ops:
  7.2 0.0 copy-start
  7.2 1.0 convert_reduce_fusion
  8.2 0.7 fusion.15
  8.9 5.7 %scatter_fusion = s32[32,4]{0,1:T(4,128)S(1)} fusion(s32[32,4]{0,1:T(4,128)S(1)} %broadcast.75, s32[64]{0:T(128)S(1)} %get-tuple-element.2, s32[64]{0:T(128)} %param.10), kind=kCustom, calls=%fused_computation.2 | custom fusion | bytes 1280 | tf_op jit(solution)/shard_map/scatter | solution.py:65
  14.6 0.7 copy.33
  15.3 8.6 %all-to-all-start = ((s32[32,1,4]{2,1,0:T(1,128)}), s32[32,1,4]{2,1,0:T(1,128)S(1)}, u32[]{:S(2)}, u32[]{:S(2)}) async-start(s32[32,1,4]{2,1,0:T(1,128)} %copy.33), calls=%async_computation | async-start | bytes 32768 | tf_op jit(solution)/shard_map/all_to_all | solution.py:68
  23.9 9.1 %fusion = bf16[8,8,8,8,128]{4,3,2,1,0:T(8,128)(2,1)S(1)} fusion(bf16[8,64,1024]{2,1,0:T(8,128)(2,1)} %param.7, bf16[8,1024,1024]{2,1,0:T(8,128)(2,1)} %param.8), kind=kOutput, calls=%fused_computation.11 | convolution fusion | flops 1074266112 | bytes 18874368 | tf_op jit(solution)/shard_map/skl,slm->skm/dot_general | solution.py:14
  33.0 1.3 copy.63
  34.3 1.9 broadcast.81.clone
  36.2 0.0 copy-start.2
  36.2 9.8 %scatter_fusion.1 = bf16[32,4,64,128]{3,2,1,0:T(8,128)(2,1)} fusion(bf16[32,4,64,128]{3,2,1,0:T(8,128)(2,1)} %broadcast.81.clone, s32[64]{0:T(128)S(1)} %get-tuple-element.2, bf16[64,64,128]{2,1,0:T(8,128)(2,1)} %bitcast.89), kind=kCustom, calls=%fused_computation.3 | custom fusion | bytes 3146240 | tf_op jit(solution)/shard_map/scatter | solution.py:40
  46.0 0.0 all-to-all-done
  46.0 7.5 %all-to-all-start.1 = ((bf16[32,4,64,128]{3,2,1,0:T(8,128)(2,1)}), bf16[32,4,64,128]{3,2,1,0:T(8,128)(2,1)}, u32[]{:S(2)}, u32[]{:S(2)}) async-start(bf16[32,4,64,128]{3,2,1,0:T(8,128)(2,1)} %scatter_fusion.1), calls=%async_computation.1 | async-start | bytes 4194304 | tf_op jit(solution)/shard_map/all_to_all | solution.py:67
  53.5 0.0 all-gather.3.cloned.1.call-start
  53.5 0.0 copy-done.2
  53.5 0.5 broadcast.184
  54.0 0.7 reduce.3
  54.7 0.1 reshape.115
  54.9 27.0 %all-to-all-done.1 = bf16[32,4,64,128]{3,2,1,0:T(8,128)(2,1)} async-done(((bf16[32,4,64,128]{3,2,1,0:T(8,128)(2,1)}), bf16[32,4,64,128]{3,2,1,0:T(8,128)(2,1)}, u32[]{:S(2)}, u32[]{:S(2)}) %all-to-all-start.1) | async-done | bytes 2097184 | tf_op jit(solution)/shard_map/all_to_all | solution.py:67
  81.8 4.0 %bitcast_convert_fusion.1 = f32[128,64,128]{2,1,0:T(8,128)} fusion(bf16[32,4,64,128]{3,2,1,0:T(8,128)(2,1)} %all-to-all-done.1), kind=kLoop, calls=%fused_computation.8 | loop fusion | flops 1048576 | bytes 6291456 | tf_op jit(solution)/shard_map/convert_element_type | solution.py:45
  85.8 13.5 %scatter_fusion.2 = f32[16,64,128]{2,1,0:T(8,128)S(1)} fusion(f32[16,64,128]{2,1,0:T(8,128)S(1)} %broadcast.74.clone, s32[128]{0:T(128)S(1)} %fusion.14, f32[128,64,128]{2,1,0:T(8,128)} %bitcast_convert_fusion.1), kind=kCustom, calls=%fused_computation.4 | custom fusion | flops 1048576 | bytes 12583424 | tf_op jit(solution)/shard_map/scatter-add | solution.py:46
  99.4 3.8 %fusion.7 = f32[64,1024]{1,0:T(8,128)} fusion(bf16[2048,1024]{1,0:T(8,128)(2,1)} %param.12, f32[2048]{0:T(1024)S(1)} %add_divide_fusion, f32[16,64,128]{2,1,0:T(8,128)S(1)} %scatter_fusion.2), kind=kOutput, calls=%fused_computation.23 | convolution fusion | flops 268697600 | bytes 4988928 | tf_op jit(solution)/shard_map/dot_general | solution.py:71
  103.1 0.0 all-gather.3.cloned.1.call-update
  103.2 0.1 copy.37
  103.3 0.1 copy.38
  103.3 0.1 reshape.129
  103.5 51.5 %all-gather.3.cloned.1.call-done = f32[2048,1024]{1,0:T(8,128)} async-done(((f32[64,1024]{1,0:T(8,128)}), f32[2048,1024]{1,0:T(8,128)}) %all-gather.3.cloned.1.call-update) | async-done | bytes 8388624 | tf_op jit(solution)/shard_map/all_gather | solution.py:10
  155.0 4.0 %reduce_sum.22 = bf16[64,1024]{1,0:T(8,128)(2,1)S(1)} reduce(f32[32,64,1024]{2,1,0:T(8,128)} %bitcast.86, f32[]{:T(128)} %constant.7.clone.1), dimensions={0}, to_apply=%region_4.0 | reduce | flops 2031616 | bytes 8519684 | tf_op jit(solution)/shard_map/reduce_sum | solution.py:10
  159.0 0.0 copy-done
  159.0 3.9 %fusion.2 = f32[64,2048]{1,0:T(8,128)S(1)} fusion(bf16[2048,1024]{1,0:T(8,128)(2,1)} %param.12, bf16[1024,1024]{1,0:T(8,128)(2,1)S(1)} %copy-done, bf16[64,1024]{1,0:T(8,128)(2,1)S(1)} %reduce_sum.22), kind=kOutput, calls=%fused_computation.14 | convolution fusion | flops 402718720 | bytes 6946816 | tf_op jit(solution)/shard_map/dot_general | solution.py:76
  163.0 0.0 copy-start.1
  163.0 2.1 gather_fusion
  165.1 33.7 %all_to_all.27 = bf16[32,4,64,128]{3,2,1,0:T(8,128)(2,1)} all-to-all(bf16[32,4,64,128]{3,2,1,0:T(8,128)(2,1)} %bitcast.87), channel_id=1, replica_groups=mesh['sub'=32,'rep'=4] {'sub'}, dimensions={0} | all-to-all | bytes 4194304 | tf_op jit(solution)/shard_map/all_to_all | solution.py:82
  198.9 0.0 copy-done.1
  198.9 3.3 %gather_fusion.1 = bf16[64,64,128]{2,1,0:T(8,128)(2,1)} fusion(bf16[32,4,64,128]{3,2,1,0:T(8,128)(2,1)} %all_to_all.27, s32[64]{0:T(128)S(1)} %bitcast.91), kind=kCustom, calls=%fused_computation.1 | custom fusion | bytes 2097664 | tf_op jit(solution)/shard_map/gather | solution.py:83
  202.2 9.1 %fusion.1 = bf16[8,8,8,8,128]{4,3,2,1,0:T(8,128)(2,1)S(1)} fusion(bf16[8,1024,1024]{2,1,0:T(8,128)(2,1)} %param.8, bf16[8,8,8,8,128]{4,3,2,1,0:T(8,128)(2,1)} %bitcast.90), kind=kOutput, calls=%fused_computation.12 | convolution fusion | flops 1074266112 | bytes 18874368 | tf_op jit(solution)/shard_map/skl,slm->skm/dot_general | solution.py:14
  211.3 1.3 copy.62
  212.6 1.9 broadcast.81
  214.5 9.8 %scatter_fusion.3 = bf16[32,4,64,128]{3,2,1,0:T(8,128)(2,1)} fusion(bf16[32,4,64,128]{3,2,1,0:T(8,128)(2,1)} %broadcast.81, s32[64]{0:T(128)S(1)} %get-tuple-element.2, bf16[64,64,128]{2,1,0:T(8,128)(2,1)} %bitcast.88), kind=kCustom, calls=%fused_computation.5 | custom fusion | bytes 3146240 | tf_op jit(solution)/shard_map/scatter | solution.py:40
  224.3 32.1 %all_to_all.28 = bf16[32,4,64,128]{3,2,1,0:T(8,128)(2,1)S(1)} all-to-all(bf16[32,4,64,128]{3,2,1,0:T(8,128)(2,1)} %scatter_fusion.3), channel_id=1, replica_groups=mesh['sub'=32,'rep'=4] {'sub'}, dimensions={0} | all-to-all | bytes 4194304 | tf_op jit(solution)/shard_map/all_to_all | solution.py:86
  256.4 2.5 bitcast_convert_fusion
  259.0 13.5 %scatter_fusion.4 = f32[16,64,128]{2,1,0:T(8,128)S(1)} fusion(f32[16,64,128]{2,1,0:T(8,128)S(1)} %broadcast.74, s32[128]{0:T(128)S(1)} %fusion.14, f32[128,64,128]{2,1,0:T(8,128)} %bitcast_convert_fusion), kind=kCustom, calls=%fused_computation.6 | custom fusion | flops 1048576 | bytes 12583424 | tf_op jit(solution)/shard_map/scatter-add | solution.py:46
  272.5 0.9 fusion.5
  (8 shorter events, 0.2 us)
Async XLA Ops:
  7.2 151.8 %copy-start = (bf16[1024,1024]{1,0:T(8,128)(2,1)S(1)}, bf16[1024,1024]{1,0:T(8,128)(2,1)}, u32[]{:S(2)}) copy-start(bf16[1024,1024]{1,0:T(8,128)(2,1)} %param.13) | copy-start | bytes 6291460
  15.3 30.7 %all-to-all-start = ((s32[32,1,4]{2,1,0:T(1,128)}), s32[32,1,4]{2,1,0:T(1,128)S(1)}, u32[]{:S(2)}, u32[]{:S(2)}) async-start(s32[32,1,4]{2,1,0:T(1,128)} %copy.33), calls=%async_computation | async-start | bytes 32768 | tf_op jit(solution)/shard_map/all_to_all | solution.py:68
  36.2 17.3 %copy-start.2 = (s32[2048]{0:T(1024)S(1)}, s32[2048]{0:T(1024)}, u32[]{:S(2)}) copy-start(s32[2048]{0:T(1024)} %param.11) | copy-start | bytes 24580
  46.0 35.8 %all-to-all-start.1 = ((bf16[32,4,64,128]{3,2,1,0:T(8,128)(2,1)}), bf16[32,4,64,128]{3,2,1,0:T(8,128)(2,1)}, u32[]{:S(2)}, u32[]{:S(2)}) async-start(bf16[32,4,64,128]{3,2,1,0:T(8,128)(2,1)} %scatter_fusion.1), calls=%async_computation.1 | async-start | bytes 4194304 | tf_op jit(solution)/shard_map/all_to_all | solution.py:67
  53.5 101.5 %all-gather.3.cloned.1.call-start = ((), (), s32[]{:S(2)}) async-start(), calls=%async_computation.4 | async-start | bytes 8650752 | tf_op jit(solution)/shard_map/all_gather | solution.py:10
  163.0 35.9 %copy-start.1 = (f32[64,2048]{1,0:T(8,128)}, f32[64,2048]{1,0:T(8,128)S(1)}, u32[]{:S(2)}) copy-start(f32[64,2048]{1,0:T(8,128)S(1)} %fusion.2) | copy-start | bytes 1572868
Sparse Core Ops, SparseCore 0:
  103.3 51.6 all-gather.2
